TPU v7x, 32 devices: a whole 2x2x4 slice. The times are simulated.
32 devices in a mesh: bands: 2 (over core), gy: 4 (over y, x), gz: 4 (over z).
Axes of the slice: x: 2, y: 2, z: 4, core: 2. Of those that a mesh axis runs over, the one named last changes fastest.
Arguments:
- orbitals: float32 [4, 64, 64, 128], P('bands', 'gy', 'gz'), may hold values from -6 to 6
- orbital_shift: float32 [4], P('bands'), may hold values from 0.1 to 1
- occupation: float32 [4], P('bands'), may hold values from 0.125 to 0.5
- potential: float32 [64, 64, 128], P('gy', 'gz'), may hold values from 0.1 to 2
- perturbation: float32 [64, 64, 128], P('gy', 'gz'), may hold values from -6 to 6
- kernel: float32 [64, 64, 128], P('gy', 'gz'), may hold values from 0.2 to 1
Outputs:
- response: float32 [4, 64, 64, 128], P('bands', 'gy', 'gz')
- density: float32 [64, 64, 128], P('gy', 'gz', 'bands')
All inputs are finite; a program needn't handle non-finite values.
Results may differ from a plain program's by a relative error of at most 0.00002.
Values sent between devices are 32-bit elements; how exact they have to be, the bound alone decides.
A program may use at most 64 MiB of HBM per device.

v0:
```python
import functools

import jax
import jax.numpy as jnp
from jax import lax
from jax.experimental import pallas as pl
from jax.experimental.pallas import tpu as pltpu
from jax.sharding import PartitionSpec as P

SWEEPS = 4
OUTER = 2
RELAX = 0.8
MESH = pl.DeviceIdType.MESH
CHUNK = 32


def chunks(start, stop, size):
    row = start
    while row < stop:
        step = min(size, stop - row)
        yield row, step
        row += step


def kernel(counts, shift_ref, occ_ref, orb_hbm, pot_hbm, pert_hbm, kern_hbm,
           resp_hbm, dens_ref,
           orb_ref, pp_ref, kern_ref, respv,
           zs1, yr1, zr1, zsu, yr2, zr2, resp0, part, partr, part2, partr2, hp, hpr,
           obuf, fbuf, rbuf, sbuf, ua, ub, pbuf,
           send1, recv1, send2, recv2, sendb, recvb, local_sem):
    nb, gy, gz = counts
    w = SWEEPS
    orbs, ny, nz, nx = orb_ref.shape
    zp = nz + 2 * w
    yp_count = ny + 2 * w
    base = zp + 8
    b = lax.axis_index("bands")
    y = lax.axis_index("gy")
    z = lax.axis_index("gz")
    parity = lax.rem(b, 2)
    ysides = {1: lax.rem(y + 1, gy), -1: lax.rem(y + gy - 1, gy), 0: y}
    zsides = {1: lax.rem(z + 1, gz), -1: lax.rem(z + gz - 1, gz), 0: z}

    def device(dy, dz):
        return {"bands": b, "gy": ysides[dy], "gz": zsides[dz]}

    faces = ((0, 1), (0, -1), (1, 0), (-1, 0))
    corners = ((1, 1), (1, -1), (-1, 1), (-1, -1))
    barrier = pltpu.get_barrier_semaphore()
    for dy, dz in corners + faces:
        pl.semaphore_signal(barrier, inc=1, device_id=device(dy, dz), device_id_type=MESH)
    for d in range(1, nb):
        pl.semaphore_signal(barrier, inc=1, device_id={"bands": lax.rem(b + d, nb), "gy": y, "gz": z},
                            device_id_type=MESH)
    loads = [pltpu.make_async_copy(src, dst, local_sem.at[i]) for i, (src, dst) in enumerate((
        (pert_hbm, pp_ref.at[0]), (pot_hbm, pp_ref.at[1]), (orb_hbm, orb_ref), (kern_hbm, kern_ref)))]
    for copy in loads:
        copy.start()

    def pack(dst, slot, value_of):
        for row in range(ny):
            dst[0, slot, row * w:(row + 1) * w, :] = value_of(row, 0)
            dst[1, slot, row * w:(row + 1) * w, :] = value_of(row, nz - w)

    def border(packed, slots, own, yr, zr, send, recv, at):
        made = {}
        for dy, dz in faces + corners:
            n = at + len(made)
            if dz:
                side, into = (1, 0) if dz == 1 else (0, 1)
                if dy == 1:
                    src, dst, size = (ny - w) * w, 8, w * w
                elif dy == -1:
                    src, dst, size = 0, 8 + (w + ny) * w, w * w
                else:
                    src, dst, size = 0, 8 + w * w, ny * w
                source = packed.at[side, slots, pl.ds(src, size)]
                target = zr.at[into, slots, pl.ds(dst, size)]
            else:
                into, start = (0, ny - w) if dy == 1 else (1, 0)
                source = own(start)
                target = yr.at[into, slots]
            made[dy, dz] = pltpu.make_async_remote_copy(
                src_ref=source, dst_ref=target, send_sem=send.at[n], recv_sem=recv.at[n],
                device_id=device(dy, dz), device_id_type=MESH)
        return made

    pslot, vslot, kslot = orbs, orbs + 1, orbs + 2
    mine = orbs + parity
    loads[0].wait()
    pack(zs1, pslot, lambda row, at: pp_ref[0, row, at:at + w, :])
    loads[1].wait()
    pack(zs1, vslot, lambda row, at: pp_ref[1, row, at:at + w, :])
    loads[2].wait()
    for o in range(orbs):
        pack(zs1, o, lambda row, at, o=o: orb_ref[o, row, at:at + w, :])
    loads[3].wait()
    pack(zs1, kslot, lambda row, at: kern_ref[row, at:at + w, :])
    pl.semaphore_wait(barrier, len(faces + corners) + nb - 1)

    own_mine = border(zs1, mine, lambda start: pp_ref.at[parity, pl.ds(start, w)], yr1, zr1, send1, recv1, 0)
    own_orbs = border(zs1, pl.ds(0, orbs), lambda start: orb_ref.at[:, pl.ds(start, w)], yr1, zr1, send1, recv1, 8)
    for key in corners:
        own_orbs[key].start()
    for key in corners + faces:
        own_mine[key].start()
    for key in faces:
        own_orbs[key].start()

    sign = 1 - 2 * parity
    partner = {"bands": b + sign, "gy": y, "gz": z}
    ysend = lax.rem(y + gy + sign, gy)
    zsend = lax.rem(z + gz + sign, gz)
    source_row = pl.multiple_of((1 - parity) * ((ny - w) * w), 8)
    target_row = pl.multiple_of(8 + parity * ((w + ny) * w), 8)
    moves = (
        (zs1.at[1, kslot, pl.ds(source_row, w * w)], zr1.at[0, kslot, pl.ds(target_row, w * w)], ysend, zsides[1]),
        (zs1.at[0, kslot, pl.ds(source_row, w * w)], zr1.at[1, kslot, pl.ds(target_row, w * w)], ysend, zsides[-1]),
        (zs1.at[1 - parity, kslot], zr1.at[parity, kslot, pl.ds(8 + w * w, ny * w)], y, zsend),
        (kern_ref.at[pl.ds((1 - parity) * (ny - w), w)], yr1.at[parity, kslot], ysend, z),
    )
    kern_copies = [pltpu.make_async_remote_copy(
        src_ref=src, dst_ref=dst, send_sem=send1.at[16 + i], recv_sem=recv1.at[16 + i],
        device_id={"bands": b, "gy": ty, "gz": tz}, device_id_type=MESH)
        for i, (src, dst, ty, tz) in enumerate(moves)]
    kern_relays = [pltpu.make_async_remote_copy(
        src_ref=dst, dst_ref=dst, send_sem=send1.at[20 + i], recv_sem=recv1.at[20 + i],
        device_id=partner, device_id_type=MESH) for i, (_, dst, _, _) in enumerate(moves)]
    for copy in kern_copies:
        copy.start()
    for key in faces + corners:
        own_mine[key].wait_recv()
    relays = [pltpu.make_async_remote_copy(
        src_ref=ref.at[:, mine], dst_ref=ref.at[:, mine], send_sem=send1.at[24 + i], recv_sem=recv1.at[24 + i],
        device_id=partner, device_id_type=MESH) for i, ref in enumerate((yr1, zr1))]
    for copy in relays:
        copy.start()
    for copy in relays:
        copy.wait_recv()
    for key in faces + corners:
        own_orbs[key].wait_recv()

    low = lax.broadcasted_iota(jnp.int32, (8, nx), 0) < w

    def tiles():
        for yp in range(-1, yp_count):
            if yp >= 0:
                yield yp, 0, base + zp * yp, nz
            yield yp, 1, base + zp * yp + nz, 2 * w

    def padded(own, yr, zr, slot, yp, third):
        if third:
            row = 8 + w * yp
            return jnp.where(low, zr[1, slot, row:row + 2 * w, :], zr[0, slot, row:row + 2 * w, :])
        if yp < w:
            return yr[0, slot, yp]
        if yp >= w + ny:
            return yr[1, slot, yp - w - ny]
        return own(yp - w)

    for yp, third, row, size in tiles():
        pv = padded(lambda r: pp_ref[0, r], yr1, zr1, pslot, yp, third)
        vv = padded(lambda r: pp_ref[1, r], yr1, zr1, vslot, yp, third)
        pbuf[row:row + size, :] = pv
        for o in range(orbs):
            ov = padded(lambda r: orb_ref[o, r], yr1, zr1, o, yp, third)
            obuf[o, row:row + size, :] = ov
            fbuf[o, row:row + size, :] = ov * pv
            rbuf[o, row:row + size, :] = (RELAX / 60.0) / (32.0 / 15.0 + (vv + shift_ref[o]))

    def span(k):
        return base + zp * (k - 1) + nz, base + zp * (yp_count - k)

    def lane_sum(v):
        return pltpu.roll(v, 1, 1) + pltpu.roll(v, nx - 1, 1)

    def source60(o, row, size):
        def at(shift):
            return fbuf[o, row + shift:row + shift + size, :]
        f = at(0)
        return -30.0 * f - 5.0 * (lane_sum(f) + (at(zp) + at(-zp)) + (at(1) + at(-1)))

    def relaxed(u, o, row, size, source):
        def at(shift):
            return u[o, row + shift:row + shift + size, :]
        c = at(0)
        faces = (at(zp) + at(-zp)) + (at(1) + at(-1))
        corners = (at(zp + 1) + at(zp - 1)) + (at(1 - zp) + at(-1 - zp))
        off = 14.0 * faces + 3.0 * corners + lane_sum(14.0 * c + 3.0 * faces + corners)
        return 0.2 * c + rbuf[o, row:row + size, :] * (source + off)

    def sweep(src, dst, k):
        for o in range(orbs):
            for row, size in chunks(*span(k), CHUNK):
                dst[o, row:row + size, :] = relaxed(src, o, row, size, sbuf[o, row:row + size, :])

    def last(src, dst, part_ref):
        for o in range(orbs):
            for r in range(ny):
                row = base + zp * (r + w)
                value = relaxed(src, o, row, nz, sbuf[o, row:row + nz, :])
                dst[o, r] = value
                term = occ_ref[o] * obuf[o, row:row + nz, :] * value
                part_ref[r] = term if o == 0 else part_ref[r] + term

    def band_copies(src, dst, at):
        return [pltpu.make_async_remote_copy(
            src_ref=src, dst_ref=dst.at[d - 1], send_sem=sendb.at[at + d - 1], recv_sem=recvb.at[at + d - 1],
            device_id={"bands": lax.rem(b + d, nb), "gy": y, "gz": z}, device_id_type=MESH)
            for d in range(1, nb)]

    for o in range(orbs):
        for row, size in chunks(*span(1), CHUNK):
            s = source60(o, row, size)
            sbuf[o, row:row + size, :] = s
            ua[o, row:row + size, :] = rbuf[o, row:row + size, :] * s
    sweep(ua, ub, 2)
    sweep(ub, ua, 3)
    last(ua, resp0, part)

    bands = band_copies(part, partr, 0)
    for copy in bands:
        copy.start()
    for o in range(orbs):
        pack(zsu, o, lambda row, at, o=o: resp0[o, row, at:at + w, :])
    second = border(zsu, pl.ds(0, orbs), lambda start: resp0.at[:, pl.ds(start, w)], yr2, zr2, send2, recv2, 0)
    for key in corners + faces:
        second[key].start()
    for copy in bands:
        copy.wait_recv()
    for copy in kern_copies:
        copy.wait_recv()
    for copy in kern_relays:
        copy.start()
    for r in range(ny):
        total = part[r]
        for d in range(nb - 1):
            total = total + partr[d, r]
        row = base + zp * (r + w)
        cv = pbuf[row:row + nz, :] + kern_ref[r] * total
        for o in range(orbs):
            fbuf[o, row:row + nz, :] = obuf[o, row:row + nz, :] * cv
            ua[o, row:row + nz, :] = resp0[o, r]
    for copy in kern_relays:
        copy.wait_recv()
    for key in faces + corners:
        second[key].wait_recv()

    rim, at = [], 0
    for yp, third, row, size in tiles():
        if third or yp < w or yp >= w + ny:
            rim.append((yp, third, row, size, at))
            at += size
    for yp, third, row, size, at in rim:
        term = None
        for o in range(orbs):
            value = padded(None, yr2, zr2, o, yp, third)
            ua[o, row:row + size, :] = value
            more = occ_ref[o] * obuf[o, row:row + size, :] * value
            term = more if term is None else term + more
        hp[at:at + size, :] = term
    rims = band_copies(hp, hpr, 2 * (nb - 1))
    for copy in rims:
        copy.start()
    for copy in rims:
        copy.wait_recv()
    for yp, third, row, size, at in rim:
        total = hp[at:at + size, :]
        for d in range(nb - 1):
            total = total + hpr[d, at:at + size, :]
        cv = pbuf[row:row + size, :] + padded(None, yr1, zr1, kslot, yp, third) * total
        for o in range(orbs):
            fbuf[o, row:row + size, :] = obuf[o, row:row + size, :] * cv
    for o in range(orbs):
        for row, size in chunks(*span(1), CHUNK):
            s = source60(o, row, size)
            sbuf[o, row:row + size, :] = s
            ub[o, row:row + size, :] = relaxed(ua, o, row, size, s)
    sweep(ub, ua, 2)
    sweep(ua, ub, 3)
    last(ub, respv, part2)
    bands2 = band_copies(part2, partr2, nb - 1)
    for copy in bands2:
        copy.start()
    out = pltpu.make_async_copy(respv, resp_hbm, local_sem.at[4])
    out.start()
    for copy in bands2:
        copy.wait_recv()
    width = nx // nb
    for r in range(ny):
        total = part2[r]
        for d in range(nb - 1):
            total = total + partr2[d, r]
        dens_ref[r] = pltpu.roll(total, lax.rem(nx - b * width, nx), 1)[:, :width]
    out.wait()
    for group in (own_mine, own_orbs, second):
        for key in faces + corners:
            group[key].wait_send()
    for copy in relays + kern_copies + kern_relays + bands + rims + bands2:
        copy.wait_send()


def on_device(counts, orbitals, orbital_shift, occupation, potential, perturbation, kernel_field):
    nb = counts[0]
    orbs, ny, nz, nx = orbitals.shape
    w = SWEEPS
    zp, yp_count = nz + 2 * w, ny + 2 * w
    rows = (nz + 2 * w) * (ny + 2 * w + 1) + 8 + 16
    rows = (rows + 7) // 8 * 8
    zrows = 8 + w * (ny + 2 * w) + 8
    f32 = jnp.float32
    vmem = lambda *shape: pltpu.VMEM(shape, f32)
    wide = vmem(orbs, rows, nx)
    tile = vmem(ny, nz, nx)
    dma = lambda n: pltpu.SemaphoreType.DMA((n,))
    rim_rows = (zp * yp_count - ny * nz) + 8
    scratch = [
        vmem(orbs, ny, nz, nx), vmem(2, ny, nz, nx), tile, vmem(orbs, ny, nz, nx),
        vmem(2, orbs + 3, ny * w, nx), vmem(2, orbs + 3, w, nz, nx), vmem(2, orbs + 3, zrows, nx),
        vmem(2, orbs, ny * w, nx), vmem(2, orbs, w, nz, nx), vmem(2, orbs, zrows, nx),
        vmem(orbs, ny, nz, nx), tile, vmem(nb - 1, ny, nz, nx), tile, vmem(nb - 1, ny, nz, nx),
        vmem(rim_rows, nx), vmem(nb - 1, rim_rows, nx),
        wide, wide, wide, wide, wide, wide, vmem(rows, nx),
        dma(26), dma(26), dma(8), dma(8), dma(3 * (nb - 1)), dma(3 * (nb - 1)), dma(5),
    ]
    spec = pl.BlockSpec(memory_space=pltpu.VMEM)
    hbm = pl.BlockSpec(memory_space=pl.ANY)
    smem = pl.BlockSpec(memory_space=pltpu.SMEM)
    return pl.pallas_call(
        functools.partial(kernel, counts),
        out_shape=(jax.ShapeDtypeStruct(orbitals.shape, f32),
                   jax.ShapeDtypeStruct((ny, nz, nx // nb), f32)),
        in_specs=[smem, smem, hbm, hbm, hbm, hbm],
        out_specs=(hbm, spec),
        scratch_shapes=scratch,
        compiler_params=pltpu.CompilerParams(collective_id=0, has_side_effects=True),
    )(orbital_shift, occupation, orbitals, potential, perturbation, kernel_field)


def solution(mesh):
    counts = (mesh.shape["bands"], mesh.shape["gy"], mesh.shape["gz"])
    placed = (
        P("bands", "gy", "gz", None),
        P("bands"),
        P("bands"),
        P("gy", "gz", None),
        P("gy", "gz", None),
        P("gy", "gz", None),
    )
    return jax.shard_map(
        functools.partial(on_device, counts),
        mesh=mesh,
        in_specs=placed,
        out_specs=(P("bands", "gy", "gz", None), P("gy", "gz", "bands")),
        check_vma=False,
    )
```

profile of v0, /device:TPU:0, one launch (start us, length us, event | category | flops | bytes accessed | tf_op | source)
XLA Modules:
  0.0 31.8 jit_solution(94059542139605816)
XLA Ops:
  0.6 28.8 %shard_map.77 = (f32[2,16,16,128]{3,2,1,0:T(8,128)}, f32[16,16,64]{2,1,0:T(8,128)}) custom-call(f32[2]{0:T(128)} %shift_ref.1, f32[2]{0:T(128)} %occ_ref.1, f32[2,16,16,128]{3,2,1,0:T(8,128)} %orb_hbm.1, f32[16,16,128]{2,1,0:T(8,128)} %pot_hbm.1, f32[16,16,128]{2,1,0:T(8,128)} %pert_hbm.1, f32[16,16,128]{2,1,0:T(8,128)} %kern_hbm.1), custom_call_target="tpu_custom_call" | custom-call | tf_op jit(solution)/shard_map/pallas_call | solution.py:329
  29.4 0.0 copy-start
  29.4 1.7 %copy.10 = f32[2,16,16,128]{3,2,1,0:T(8,128)} copy(f32[2,16,16,128]{3,2,1,0:T(8,128)} %get-tuple-element.4) | data formatting | bytes 524288
  31.1 0.0 copy-done
  31.1 0.7 %copy.11 = f32[16,16,64]{2,1,0:T(8,128)} copy(f32[16,16,64]{2,1,0:T(8,128)S(1)} %copy-done) | data formatting | bytes 131072
Async XLA Ops:
  29.4 1.7 %copy-start = (f32[16,16,64]{2,1,0:T(8,128)S(1)}, f32[16,16,64]{2,1,0:T(8,128)}, u32[]{:S(2)}) copy-start(f32[16,16,64]{2,1,0:T(8,128)} %get-tuple-element.5) | copy-start | bytes 196612
where the time goes:
time: 31.9 us; the launch traced here: 31.8 us
  Pallas kernels  28.8 us (90%)
  local copies, waits for them, and re-layouts  2.36 us (7%)
  between operations  0.65 us (2%)
    pallas_call x1, Pallas kernels, on_device(): pl.pallas_call(functools.partial(kernel, counts), out_shape=(jax.ShapeDty...  28.8 us
    unnamed x4, local copies, waits for them, and re-layouts  2.36 us

commit v1 on v0

--- a/solution.py
+++ b/solution.py
@@ -12,6 +12,7 @@
 RELAX = 0.8
 MESH = pl.DeviceIdType.MESH
 CHUNK = 32
+GRANT = 24 * 1024 * 1024
 
 
 def chunks(start, stop, size):
@@ -22,9 +23,9 @@
         row += step
 
 
-def kernel(counts, shift_ref, occ_ref, orb_hbm, pot_hbm, pert_hbm, kern_hbm,
-           resp_hbm, dens_ref,
-           orb_ref, pp_ref, kern_ref, respv,
+def kernel(counts, shift_hbm, occ_hbm, orb_hbm, pot_hbm, pert_hbm, kern_hbm,
+           respv, dens_ref,
+           shift_ref, occ_ref, orb_ref, pp_ref, kern_ref,
            zs1, yr1, zr1, zsu, yr2, zr2, resp0, part, partr, part2, partr2, hp, hpr,
            obuf, fbuf, rbuf, sbuf, ua, ub, pbuf,
            send1, recv1, send2, recv2, sendb, recvb, local_sem):
@@ -53,7 +54,8 @@
         pl.semaphore_signal(barrier, inc=1, device_id={"bands": lax.rem(b + d, nb), "gy": y, "gz": z},
                             device_id_type=MESH)
     loads = [pltpu.make_async_copy(src, dst, local_sem.at[i]) for i, (src, dst) in enumerate((
-        (pert_hbm, pp_ref.at[0]), (pot_hbm, pp_ref.at[1]), (orb_hbm, orb_ref), (kern_hbm, kern_ref)))]
+        (pert_hbm, pp_ref.at[0]), (pot_hbm, pp_ref.at[1]), (orb_hbm, orb_ref), (kern_hbm, kern_ref),
+        (shift_hbm, shift_ref), (occ_hbm, occ_ref)))]
     for copy in loads:
         copy.start()
 
@@ -96,6 +98,8 @@
         pack(zs1, o, lambda row, at, o=o: orb_ref[o, row, at:at + w, :])
     loads[3].wait()
     pack(zs1, kslot, lambda row, at: kern_ref[row, at:at + w, :])
+    loads[4].wait()
+    loads[5].wait()
     pl.semaphore_wait(barrier, len(faces + corners) + nb - 1)
 
     own_mine = border(zs1, mine, lambda start: pp_ref.at[parity, pl.ds(start, w)], yr1, zr1, send1, recv1, 0)
@@ -282,8 +286,6 @@
     bands2 = band_copies(part2, partr2, nb - 1)
     for copy in bands2:
         copy.start()
-    out = pltpu.make_async_copy(respv, resp_hbm, local_sem.at[4])
-    out.start()
     for copy in bands2:
         copy.wait_recv()
     width = nx // nb
@@ -292,12 +294,20 @@
         for d in range(nb - 1):
             total = total + partr2[d, r]
         dens_ref[r] = pltpu.roll(total, lax.rem(nx - b * width, nx), 1)[:, :width]
-    out.wait()
     for group in (own_mine, own_orbs, second):
         for key in faces + corners:
             group[key].wait_send()
     for copy in relays + kern_copies + kern_relays + bands + rims + bands2:
         copy.wait_send()
+
+
+def store(resp_ref, dens_ref, resp_hbm, dens_hbm, sem):
+    copies = [pltpu.make_async_copy(src, dst, sem.at[i])
+              for i, (src, dst) in enumerate(((resp_ref, resp_hbm), (dens_ref, dens_hbm)))]
+    for copy in copies:
+        copy.start()
+    for copy in copies:
+        copy.wait()
 
 
 def on_device(counts, orbitals, orbital_shift, occupation, potential, perturbation, kernel_field):
@@ -315,26 +325,35 @@
     dma = lambda n: pltpu.SemaphoreType.DMA((n,))
     rim_rows = (zp * yp_count - ny * nz) + 8
     scratch = [
-        vmem(orbs, ny, nz, nx), vmem(2, ny, nz, nx), tile, vmem(orbs, ny, nz, nx),
+        pltpu.SMEM((orbs,), f32), pltpu.SMEM((orbs,), f32),
+        vmem(orbs, ny, nz, nx), vmem(2, ny, nz, nx), tile,
         vmem(2, orbs + 3, ny * w, nx), vmem(2, orbs + 3, w, nz, nx), vmem(2, orbs + 3, zrows, nx),
         vmem(2, orbs, ny * w, nx), vmem(2, orbs, w, nz, nx), vmem(2, orbs, zrows, nx),
         vmem(orbs, ny, nz, nx), tile, vmem(nb - 1, ny, nz, nx), tile, vmem(nb - 1, ny, nz, nx),
         vmem(rim_rows, nx), vmem(nb - 1, rim_rows, nx),
         wide, wide, wide, wide, wide, wide, vmem(rows, nx),
-        dma(26), dma(26), dma(8), dma(8), dma(3 * (nb - 1)), dma(3 * (nb - 1)), dma(5),
+        dma(26), dma(26), dma(8), dma(8), dma(3 * (nb - 1)), dma(3 * (nb - 1)), dma(6),
     ]
     spec = pl.BlockSpec(memory_space=pltpu.VMEM)
-    hbm = pl.BlockSpec(memory_space=pl.ANY)
-    smem = pl.BlockSpec(memory_space=pltpu.SMEM)
+    hbm = pl.BlockSpec(memory_space=pltpu.HBM)
+    response, density = pl.pallas_call(
+        functools.partial(kernel, counts),
+        out_shape=(pltpu.VMEM(orbitals.shape, f32), pltpu.VMEM((ny, nz, nx // nb), f32)),
+        in_specs=[hbm] * 6,
+        out_specs=(spec, spec),
+        scratch_shapes=scratch,
+        compiler_params=pltpu.CompilerParams(
+            collective_id=0, has_side_effects=True, vmem_limit_bytes=GRANT),
+    )(*(pltpu.with_memory_space_constraint(array, pltpu.HBM) for array in (
+        orbital_shift, occupation, orbitals, potential, perturbation, kernel_field)))
     return pl.pallas_call(
-        functools.partial(kernel, counts),
-        out_shape=(jax.ShapeDtypeStruct(orbitals.shape, f32),
-                   jax.ShapeDtypeStruct((ny, nz, nx // nb), f32)),
-        in_specs=[smem, smem, hbm, hbm, hbm, hbm],
-        out_specs=(hbm, spec),
-        scratch_shapes=scratch,
-        compiler_params=pltpu.CompilerParams(collective_id=0, has_side_effects=True),
-    )(orbital_shift, occupation, orbitals, potential, perturbation, kernel_field)
+        store,
+        out_shape=(jax.ShapeDtypeStruct(response.shape, f32), jax.ShapeDtypeStruct(density.shape, f32)),
+        in_specs=[spec, spec],
+        out_specs=(hbm, hbm),
+        scratch_shapes=[dma(2)],
+        compiler_params=pltpu.CompilerParams(vmem_limit_bytes=GRANT),
+    )(response, density)
 
 
 def solution(mesh):

time: 31.9 us -> 29 us (0.909)
  local copies, waits for them, and re-layouts: 2.36 us -> 0 us
  Pallas kernels: 28.8 us -> 28.2 us
    unnamed x4 -> x0, local copies, waits for them, and re-layouts: 2.36 us -> none
    pallas_call x1 -> x2, Pallas kernels: 28.8 us -> 28.2 us  [the longest x1 27.4 us: on_device(): pl.pallas_call(functools.partial(kernel, counts), out_shape=(pltpu.VMEM(o...]
where the time goes in v1:
time: 29 us; the launch traced here: 28.8 us
  Pallas kernels  28.2 us (97%)
  between operations  0.64 us (2%)
    pallas_call x1, Pallas kernels, on_device(): pl.pallas_call(functools.partial(kernel, counts), out_shape=(pltpu.VMEM(o...  27.4 us
    pallas_call x1, Pallas kernels, on_device(): pl.pallas_call(store, out_shape=(jax.ShapeDtypeStruct(response.shape, f32...  0.76 us

profile of v1, /device:TPU:0, one launch (start us, length us, event | category | flops | bytes accessed | tf_op | source)
XLA Modules:
  0.0 28.8 jit_solution(5581623188773929121)
XLA Ops:
  0.6 27.4 %shard_map.77 = (f32[2,16,16,128]{3,2,1,0:T(8,128)S(1)}, f32[16,16,64]{2,1,0:T(8,128)S(1)}) custom-call(f32[2]{0:T(128)} %shift_hbm.1, f32[2]{0:T(128)} %occ_hbm.1, f32[2,16,16,128]{3,2,1,0:T(8,128)} %orb_hbm.1, f32[16,16,128]{2,1,0:T(8,128)} %pot_hbm.1, f32[16,16,128]{2,1,0:T(8,128)} %pert_hbm.1, f32[16,16,128]{2,1,0:T(8,128)} %kern_hbm.1), custom_call_target="tpu_custom_call" | custom-call | tf_op jit(solution)/shard_map/pallas_call | solution.py:339
  28.1 0.8 %shard_map.78 = (f32[2,16,16,128]{3,2,1,0:T(8,128)}, f32[16,16,64]{2,1,0:T(8,128)}) custom-call(f32[2,16,16,128]{3,2,1,0:T(8,128)S(1)} %get-tuple-element.4.resp_ref, f32[16,16,64]{2,1,0:T(8,128)S(1)} %get-tuple-element.5.dens_ref), custom_call_target="tpu_custom_call" | custom-call | tf_op jit(solution)/shard_map/pallas_call | solution.py:349

commit v2 on v1

v2 whole, which is shorter than its diff:
```python
import functools

import jax
import jax.numpy as jnp
from jax import lax
from jax.experimental import pallas as pl
from jax.experimental.pallas import tpu as pltpu
from jax.sharding import PartitionSpec as P

SWEEPS = 4
OUTER = 2
RELAX = 0.8
MESH = pl.DeviceIdType.MESH
CHUNK = 32
GRANT = 24 * 1024 * 1024


def chunks(start, stop, size):
    row = start
    while row < stop:
        step = min(size, stop - row)
        yield row, step
        row += step


def kernel(counts, shift_hbm, occ_hbm, orb_hbm, pot_hbm, pert_hbm, kern_hbm,
           respv, dens_ref,
           shift_ref, occ_ref, orb_ref, pp_ref, kern_ref,
           zs1, yr1, zr1, cs1, zsu, yr2, zr2, resp0, part, partr, part2, partr2, hp, hpr,
           obuf, fbuf, rbuf, sbuf, ua, ub, pbuf,
           send, recv, sendb, recvb, local_sem):
    nb, gy, gz = counts
    w = SWEEPS
    orbs, ny, nz, nx = orb_ref.shape
    zp = nz + 2 * w
    yp_count = ny + 2 * w
    base = zp + 8
    block = w * w
    first, top, bottom = 8 + block, 8, 8 + (w + ny) * w
    b = lax.axis_index("bands")
    y = lax.axis_index("gy")
    z = lax.axis_index("gz")
    parity = lax.rem(b, 2)
    ysides = {1: lax.rem(y + 1, gy), -1: lax.rem(y + gy - 1, gy), 0: y}
    zsides = {1: lax.rem(z + 1, gz), -1: lax.rem(z + gz - 1, gz), 0: z}

    def device(dy, dz):
        return {"bands": b, "gy": ysides[dy], "gz": zsides[dz]}

    faces = ((0, 1), (0, -1), (1, 0), (-1, 0))
    corners = ((1, 1), (1, -1), (-1, 1), (-1, -1))
    barrier = pltpu.get_barrier_semaphore()
    for dy, dz in faces:
        pl.semaphore_signal(barrier, inc=1, device_id=device(dy, dz), device_id_type=MESH)
    for d in range(1, nb):
        pl.semaphore_signal(barrier, inc=1, device_id={"bands": lax.rem(b + d, nb), "gy": y, "gz": z},
                            device_id_type=MESH)
    loads = [pltpu.make_async_copy(src, dst, local_sem.at[i]) for i, (src, dst) in enumerate((
        (pert_hbm, pp_ref.at[0]), (pot_hbm, pp_ref.at[1]), (orb_hbm, orb_ref), (kern_hbm, kern_ref),
        (shift_hbm, shift_ref), (occ_hbm, occ_ref)))]
    for copy in loads:
        copy.start()

    copies = []

    def remote(src, dst, to):
        n = len(copies)
        copies.append(pltpu.make_async_remote_copy(
            src_ref=src, dst_ref=dst, send_sem=send.at[n], recv_sem=recv.at[n], device_id=to, device_id_type=MESH))
        return copies[-1]

    def start(group):
        for copy in group:
            copy.start()

    def arrived(group):
        for copy in group:
            copy.wait_recv()

    def pack(dst, slot, value_of):
        for row in range(ny):
            dst[0, slot, row * w:(row + 1) * w, :] = value_of(row, 0)
            dst[1, slot, row * w:(row + 1) * w, :] = value_of(row, nz - w)

    class Border:
        def __init__(self, packed, slots, fields, own, yr, zr, cs, both):
            self.fields, self.yr, self.cs = fields, yr, cs
            rest = (ny - w) * w
            z_up = lambda at, size: remote(
                packed.at[1, slots, pl.ds(at, size)], zr.at[0, slots, pl.ds(first + at, size)], device(0, 1))
            z_down = lambda at, size: remote(
                packed.at[0, slots, pl.ds(at, size)], zr.at[1, slots, pl.ds(first + at, size)], device(0, -1))
            y_up = lambda at, size: remote(
                own(ny - w, pl.ds(at, size)), yr.at[0, slots, :, pl.ds(at, size)], device(1, 0))
            y_down = lambda at, size: remote(
                own(0, pl.ds(at, size)), yr.at[1, slots, :, pl.ds(at, size)], device(-1, 0))
            self.head = (z_up(rest, block), z_down(0, block), y_up(0, 8), y_down(nz - 8, 8))
            self.rest = (z_up(0, rest), z_down(block, rest), y_up(8, nz - 8), y_down(0, nz - 8))
            moves = (
                (zr.at[0, slots, pl.ds(first + rest, block)], zr.at[0, slots, pl.ds(top, block)], device(1, 0)),
                (zr.at[1, slots, pl.ds(first, block)], zr.at[1, slots, pl.ds(bottom, block)], device(-1, 0)),
                (cs.at[0, slots], zr.at[1, slots, pl.ds(top, block)], device(0, -1)),
                (cs.at[1, slots], zr.at[0, slots, pl.ds(bottom, block)], device(0, 1)),
            )
            self.relays = [remote(*move) for move in moves]
            if both:
                self.relays += [remote(src, dst, {**to, "bands": partner["bands"]}) for src, dst, to in moves]

        def relay(self):
            arrived(self.head)
            for field in self.fields:
                for r in range(w):
                    self.cs[0, field, r * w:(r + 1) * w, :] = self.yr[0, field, r, 0:w, :]
                    self.cs[1, field, r * w:(r + 1) * w, :] = self.yr[1, field, r, nz - w:nz, :]
            start(self.relays)

        def finish(self):
            arrived(self.rest)
            arrived(self.relays)

    pslot, vslot, kslot = orbs, orbs + 1, orbs + 2
    mine = orbs + parity
    loads[0].wait()
    pack(zs1, pslot, lambda row, at: pp_ref[0, row, at:at + w, :])
    loads[1].wait()
    pack(zs1, vslot, lambda row, at: pp_ref[1, row, at:at + w, :])
    loads[2].wait()
    for o in range(orbs):
        pack(zs1, o, lambda row, at, o=o: orb_ref[o, row, at:at + w, :])
    loads[3].wait()
    pack(zs1, kslot, lambda row, at: kern_ref[row, at:at + w, :])
    loads[4].wait()
    loads[5].wait()

    sign = 1 - 2 * parity
    partner = {"bands": b + sign, "gy": y, "gz": z}
    ysend = lax.rem(y + gy + sign, gy)
    zsend = lax.rem(z + gz + sign, gz)
    far = 1 - parity
    source_row = pl.multiple_of(far * ((ny - w) * w), 8)
    end = pl.multiple_of(top + parity * ((w + ny) * w), 8)

    everyone = pl.ds(0, orbs)
    common = Border(zs1, mine, (mine,), lambda at, zs: pp_ref.at[parity, pl.ds(at, w), zs], yr1, zr1, cs1, True)
    own = Border(zs1, everyone, range(orbs), lambda at, zs: orb_ref.at[:, pl.ds(at, w), zs], yr1, zr1, cs1, False)
    shared = [remote(ref, ref, partner) for ref in (yr1.at[:, mine], zr1.at[:, mine, pl.ds(first, ny * w)])]
    kern_moves = (
        (zs1.at[1, kslot, pl.ds(source_row, block)], zr1.at[0, kslot, pl.ds(end, block)], ysend, zsides[1]),
        (zs1.at[0, kslot, pl.ds(source_row, block)], zr1.at[1, kslot, pl.ds(end, block)], ysend, zsides[-1]),
        (zs1.at[far, kslot], zr1.at[parity, kslot, pl.ds(first, ny * w)], y, zsend),
        (kern_ref.at[pl.ds(far * (ny - w), w)], yr1.at[parity, kslot], ysend, z),
    )
    kern_copies = [remote(src, dst, {"bands": b, "gy": ty, "gz": tz}) for src, dst, ty, tz in kern_moves]
    kern_shared = [remote(dst, dst, partner) for _, dst, _, _ in kern_moves]

    def direct(packed, own, yr, zr):
        made = []
        for dy, dz in corners + faces:
            if dz:
                side, into = (1, 0) if dz == 1 else (0, 1)
                if dy == 1:
                    src, dst, size = (ny - w) * w, top, block
                elif dy == -1:
                    src, dst, size = 0, bottom, block
                else:
                    src, dst, size = 0, first, ny * w
                source = packed.at[side, everyone, pl.ds(src, size)]
                target = zr.at[into, everyone, pl.ds(dst, size)]
            else:
                into, at = (0, ny - w) if dy == 1 else (1, 0)
                source = own(at)
                target = yr.at[into, everyone]
            made.append(remote(source, target, device(dy, dz)))
        return made

    second = direct(zsu, lambda at: resp0.at[:, pl.ds(at, w)], yr2, zr2)

    pl.semaphore_wait(barrier, len(faces) + nb - 1)
    start(common.head)
    start(own.head)
    start(common.rest)
    start(own.rest)
    common.relay()
    own.relay()
    arrived(common.rest)
    start(shared)
    own.finish()
    start(kern_copies)
    arrived(common.relays)
    arrived(shared)

    low = lax.broadcasted_iota(jnp.int32, (8, nx), 0) < w

    def tiles():
        for yp in range(-1, yp_count):
            if yp >= 0:
                yield yp, 0, base + zp * yp, nz
            yield yp, 1, base + zp * yp + nz, 2 * w

    def padded(own, yr, zr, slot, yp, third):
        if third:
            row = 8 + w * yp
            return jnp.where(low, zr[1, slot, row:row + 2 * w, :], zr[0, slot, row:row + 2 * w, :])
        if yp < w:
            return yr[0, slot, yp]
        if yp >= w + ny:
            return yr[1, slot, yp - w - ny]
        return own(yp - w)

    def prepare(o):
        for yp, third, row, size in tiles():
            if o == 0:
                pv = padded(lambda r: pp_ref[0, r], yr1, zr1, pslot, yp, third)
                pbuf[row:row + size, :] = pv
            else:
                pv = pbuf[row:row + size, :]
            vv = padded(lambda r: pp_ref[1, r], yr1, zr1, vslot, yp, third)
            ov = padded(lambda r: orb_ref[o, r], yr1, zr1, o, yp, third)
            obuf[o, row:row + size, :] = ov
            fbuf[o, row:row + size, :] = ov * pv
            rbuf[o, row:row + size, :] = (RELAX / 60.0) / (32.0 / 15.0 + (vv + shift_ref[o]))

    def span(k):
        return base + zp * (k - 1) + nz, base + zp * (yp_count - k)

    def lane_sum(v):
        return pltpu.roll(v, 1, 1) + pltpu.roll(v, nx - 1, 1)

    def source60(o, row, size):
        def at(shift):
            return fbuf[o, row + shift:row + shift + size, :]
        f = at(0)
        return -30.0 * f - 5.0 * (lane_sum(f) + (at(zp) + at(-zp)) + (at(1) + at(-1)))

    def relaxed(u, o, row, size, source):
        def at(shift):
            return u[o, row + shift:row + shift + size, :]
        c = at(0)
        faces = (at(zp) + at(-zp)) + (at(1) + at(-1))
        corners = (at(zp + 1) + at(zp - 1)) + (at(1 - zp) + at(-1 - zp))
        off = 14.0 * faces + 3.0 * corners + lane_sum(14.0 * c + 3.0 * faces + corners)
        if source is not None:
            off = source + off
        return 0.2 * c + rbuf[o, row:row + size, :] * off

    def sweep(src, dst, k, o):
        for row, size in chunks(*span(k), CHUNK):
            dst[o, row:row + size, :] = relaxed(src, o, row, size, sbuf[o, row:row + size, :])

    def last(src, dst, part_ref, o, rows):
        for r in rows:
            row = base + zp * (r + w)
            value = relaxed(src, o, row, nz, sbuf[o, row:row + nz, :])
            dst[o, r] = value
            term = occ_ref[o] * obuf[o, row:row + nz, :] * value
            part_ref[r] = term if o == 0 else part_ref[r] + term

    def band_copies(src, dst, at):
        return [pltpu.make_async_remote_copy(
            src_ref=src, dst_ref=dst(d - 1), send_sem=sendb.at[at + d - 1], recv_sem=recvb.at[at + d - 1],
            device_id={"bands": lax.rem(b + d, nb), "gy": y, "gz": z}, device_id_type=MESH)
            for d in range(1, nb)]

    for o in range(orbs):
        prepare(o)
        for row, size in chunks(*span(1), CHUNK):
            s = source60(o, row, size)
            sbuf[o, row:row + size, :] = s
            ua[o, row:row + size, :] = rbuf[o, row:row + size, :] * s
        sweep(ua, ub, 2, o)
        sweep(ub, ua, 3, o)
        last(ua, resp0, part, o, range(ny))
        pack(zsu, o, lambda row, at, o=o: resp0[o, row, at:at + w, :])
    start(second)

    bands = band_copies(part, lambda d: partr.at[d], 0)
    start(bands)
    arrived(kern_copies)
    start(kern_shared)
    arrived(bands)
    for r in range(ny):
        total = part[r]
        for d in range(nb - 1):
            total = total + partr[d, r]
        row = base + zp * (r + w)
        cv = pbuf[row:row + nz, :] + kern_ref[r] * total
        for o in range(orbs):
            fbuf[o, row:row + nz, :] = obuf[o, row:row + nz, :] * cv
            ua[o, row:row + nz, :] = resp0[o, r]

    rim, at = [], 0
    for yp, third, row, size in tiles():
        if third or yp < w or yp >= w + ny:
            rim.append((yp, third, row, size, at))
            at += size
    arrived(second)
    for o in range(orbs):
        for yp, third, row, size, at in rim:
            value = padded(None, yr2, zr2, o, yp, third)
            ua[o, row:row + size, :] = value
            term = occ_ref[o] * obuf[o, row:row + size, :] * value
            hp[at:at + size, :] = term if o == 0 else hp[at:at + size, :] + term
    rims = band_copies(hp, lambda d: hpr.at[d], 2 * (nb - 1))
    start(rims)
    for o in range(orbs):
        for row, size in chunks(*span(1), CHUNK):
            ub[o, row:row + size, :] = relaxed(ua, o, row, size, None)
    arrived(kern_shared)
    arrived(rims)
    for yp, third, row, size, at in rim:
        total = hp[at:at + size, :]
        for d in range(nb - 1):
            total = total + hpr[d, at:at + size, :]
        cv = pbuf[row:row + size, :] + padded(None, yr1, zr1, kslot, yp, third) * total
        for o in range(orbs):
            fbuf[o, row:row + size, :] = obuf[o, row:row + size, :] * cv
    for o in range(orbs):
        for row, size in chunks(*span(1), CHUNK):
            s = source60(o, row, size)
            sbuf[o, row:row + size, :] = s
            ub[o, row:row + size, :] = ub[o, row:row + size, :] + rbuf[o, row:row + size, :] * s
    for o in range(orbs):
        sweep(ub, ua, 2, o)
        sweep(ua, ub, 3, o)
    for o in range(orbs):
        last(ub, respv, part2, o, range(ny))
    bands2 = band_copies(part2, lambda d: partr2.at[d], nb - 1)
    start(bands2)
    width = nx // nb
    arrived(bands2)
    for r in range(ny):
        total = part2[r]
        for d in range(nb - 1):
            total = total + partr2[d, r]
        dens_ref[r] = pltpu.roll(total, lax.rem(nx - b * width, nx), 1)[:, :width]
    for copy in copies + bands + rims + bands2:
        copy.wait_send()


def store(resp_ref, dens_ref, resp_hbm, dens_hbm, sem):
    copies = [pltpu.make_async_copy(src, dst, sem.at[i])
              for i, (src, dst) in enumerate(((resp_ref, resp_hbm), (dens_ref, dens_hbm)))]
    for copy in copies:
        copy.start()
    for copy in copies:
        copy.wait()


def on_device(counts, orbitals, orbital_shift, occupation, potential, perturbation, kernel_field):
    nb = counts[0]
    orbs, ny, nz, nx = orbitals.shape
    w = SWEEPS
    zp, yp_count = nz + 2 * w, ny + 2 * w
    rows = (nz + 2 * w) * (ny + 2 * w + 1) + 8 + 16
    rows = (rows + 7) // 8 * 8
    zrows = 8 + w * (ny + 2 * w) + 8
    f32 = jnp.float32
    vmem = lambda *shape: pltpu.VMEM(shape, f32)
    wide = vmem(orbs, rows, nx)
    tile = vmem(ny, nz, nx)
    dma = lambda n: pltpu.SemaphoreType.DMA((n,))
    remotes = 16 + 12 + 2 + 8 + 8
    rim_rows = (zp * yp_count - ny * nz) + 8
    scratch = [
        pltpu.SMEM((orbs,), f32), pltpu.SMEM((orbs,), f32),
        vmem(orbs, ny, nz, nx), vmem(2, ny, nz, nx), tile,
        vmem(2, orbs + 3, ny * w, nx), vmem(2, orbs + 3, w, nz, nx), vmem(2, orbs + 3, zrows, nx),
        vmem(2, orbs + 3, w * w, nx),
        vmem(2, orbs, ny * w, nx), vmem(2, orbs, w, nz, nx), vmem(2, orbs, zrows, nx),
        vmem(orbs, ny, nz, nx), tile, vmem(nb - 1, ny, nz, nx), tile, vmem(nb - 1, ny, nz, nx),
        vmem(rim_rows, nx), vmem(nb - 1, rim_rows, nx),
        wide, wide, wide, wide, wide, wide, vmem(rows, nx),
        dma(remotes), dma(remotes), dma(3 * (nb - 1)), dma(3 * (nb - 1)), dma(6),
    ]
    spec = pl.BlockSpec(memory_space=pltpu.VMEM)
    hbm = pl.BlockSpec(memory_space=pltpu.HBM)
    response, density = pl.pallas_call(
        functools.partial(kernel, counts),
        out_shape=(pltpu.VMEM(orbitals.shape, f32), pltpu.VMEM((ny, nz, nx // nb), f32)),
        in_specs=[hbm] * 6,
        out_specs=(spec, spec),
        scratch_shapes=scratch,
        compiler_params=pltpu.CompilerParams(
            collective_id=0, has_side_effects=True, vmem_limit_bytes=GRANT),
    )(*(pltpu.with_memory_space_constraint(array, pltpu.HBM) for array in (
        orbital_shift, occupation, orbitals, potential, perturbation, kernel_field)))
    return pl.pallas_call(
        store,
        out_shape=(jax.ShapeDtypeStruct(response.shape, f32), jax.ShapeDtypeStruct(density.shape, f32)),
        in_specs=[spec, spec],
        out_specs=(hbm, hbm),
        scratch_shapes=[dma(2)],
        compiler_params=pltpu.CompilerParams(vmem_limit_bytes=GRANT),
    )(response, density)


def solution(mesh):
    counts = (mesh.shape["bands"], mesh.shape["gy"], mesh.shape["gz"])
    placed = (
        P("bands", "gy", "gz", None),
        P("bands"),
        P("bands"),
        P("gy", "gz", None),
        P("gy", "gz", None),
        P("gy", "gz", None),
    )
    return jax.shard_map(
        functools.partial(on_device, counts),
        mesh=mesh,
        in_specs=placed,
        out_specs=(P("bands", "gy", "gz", None), P("gy", "gz", "bands")),
        check_vma=False,
    )
```

time: 29 us -> 27.3 us (0.941)
  Pallas kernels: 28.2 us -> 26.5 us
    pallas_call x1, Pallas kernels: 27.4 us -> 25.8 us  [on_device(): pl.pallas_call(functools.partial(kernel, counts), out_shape=(pltpu.VMEM(o...]
where the time goes in v2:
time: 27.3 us; the launch traced here: 27.2 us
  Pallas kernels  26.5 us (97%)
  between operations  0.64 us (2%)
    pallas_call x1, Pallas kernels, on_device(): pl.pallas_call(functools.partial(kernel, counts), out_shape=(pltpu.VMEM(o...  25.8 us
    pallas_call x1, Pallas kernels, on_device(): pl.pallas_call(store, out_shape=(jax.ShapeDtypeStruct(response.shape, f32...  0.76 us

profile of v2, /device:TPU:0, one launch (start us, length us, event | category | flops | bytes accessed | tf_op | source)
XLA Modules:
  0.0 27.2 jit_solution(5329663979332293803)
XLA Ops:
  0.6 25.8 %shard_map.77 = (f32[2,16,16,128]{3,2,1,0:T(8,128)S(1)}, f32[16,16,64]{2,1,0:T(8,128)S(1)}) custom-call(f32[2]{0:T(128)} %shift_hbm.1, f32[2]{0:T(128)} %occ_hbm.1, f32[2,16,16,128]{3,2,1,0:T(8,128)} %orb_hbm.1, f32[16,16,128]{2,1,0:T(8,128)} %pot_hbm.1, f32[16,16,128]{2,1,0:T(8,128)} %pert_hbm.1, f32[16,16,128]{2,1,0:T(8,128)} %kern_hbm.1), custom_call_target="tpu_custom_call" | custom-call | tf_op jit(solution)/shard_map/pallas_call | solution.py:377
  26.4 0.8 %shard_map.78 = (f32[2,16,16,128]{3,2,1,0:T(8,128)}, f32[16,16,64]{2,1,0:T(8,128)}) custom-call(f32[2,16,16,128]{3,2,1,0:T(8,128)S(1)} %get-tuple-element.4.resp_ref, f32[16,16,64]{2,1,0:T(8,128)S(1)} %get-tuple-element.5.dens_ref), custom_call_target="tpu_custom_call" | custom-call | tf_op jit(solution)/shard_map/pallas_call | solution.py:387

commit v3 on v2

--- a/solution.py
+++ b/solution.py
@@ -77,8 +77,8 @@
         for copy in group:
             copy.wait_recv()
 
-    def pack(dst, slot, value_of):
-        for row in range(ny):
+    def pack(dst, slot, value_of, rows=range(ny)):
+        for row in rows:
             dst[0, slot, row * w:(row + 1) * w, :] = value_of(row, 0)
             dst[1, slot, row * w:(row + 1) * w, :] = value_of(row, nz - w)
 
@@ -155,7 +155,7 @@
 
     def direct(packed, own, yr, zr):
         made = []
-        for dy, dz in corners + faces:
+        for dy, dz in corners + faces[2:] + faces[:2]:
             if dz:
                 side, into = (1, 0) if dz == 1 else (0, 1)
                 if dy == 1:
@@ -175,20 +175,6 @@
 
     second = direct(zsu, lambda at: resp0.at[:, pl.ds(at, w)], yr2, zr2)
 
-    pl.semaphore_wait(barrier, len(faces) + nb - 1)
-    start(common.head)
-    start(own.head)
-    start(common.rest)
-    start(own.rest)
-    common.relay()
-    own.relay()
-    arrived(common.rest)
-    start(shared)
-    own.finish()
-    start(kern_copies)
-    arrived(common.relays)
-    arrived(shared)
-
     low = lax.broadcasted_iota(jnp.int32, (8, nx), 0) < w
 
     def tiles():
@@ -207,8 +193,13 @@
             return yr[1, slot, yp - w - ny]
         return own(yp - w)
 
-    def prepare(o):
+    def inside(yp, third):
+        return not third and w <= yp < w + ny
+
+    def prepare(o, inner):
         for yp, third, row, size in tiles():
+            if inside(yp, third) != inner:
+                continue
             if o == 0:
                 pv = padded(lambda r: pp_ref[0, r], yr1, zr1, pslot, yp, third)
                 pbuf[row:row + size, :] = pv
@@ -220,6 +211,23 @@
             fbuf[o, row:row + size, :] = ov * pv
             rbuf[o, row:row + size, :] = (RELAX / 60.0) / (32.0 / 15.0 + (vv + shift_ref[o]))
 
+    pl.semaphore_wait(barrier, len(faces) + nb - 1)
+    start(common.head)
+    start(own.head)
+    start(common.rest)
+    start(own.rest)
+    for o in range(orbs):
+        prepare(o, True)
+    common.relay()
+    own.relay()
+    start(kern_copies[2:])
+    arrived(common.rest)
+    start(shared)
+    own.finish()
+    start(kern_copies[:2])
+    arrived(common.relays)
+    arrived(shared)
+
     def span(k):
         return base + zp * (k - 1) + nz, base + zp * (yp_count - k)
 
@@ -262,16 +270,19 @@
             for d in range(1, nb)]
 
     for o in range(orbs):
-        prepare(o)
+        prepare(o, False)
         for row, size in chunks(*span(1), CHUNK):
             s = source60(o, row, size)
             sbuf[o, row:row + size, :] = s
             ua[o, row:row + size, :] = rbuf[o, row:row + size, :] * s
         sweep(ua, ub, 2, o)
         sweep(ub, ua, 3, o)
-        last(ua, resp0, part, o, range(ny))
-        pack(zsu, o, lambda row, at, o=o: resp0[o, row, at:at + w, :])
-    start(second)
+    edge = [*range(w), *range(ny - w, ny)]
+    for rows, group in ((edge, second[:6]), (range(w, ny - w), second[6:])):
+        for o in range(orbs):
+            last(ua, resp0, part, o, rows)
+            pack(zsu, o, lambda row, at, o=o: resp0[o, row, at:at + w, :], rows)
+        start(group)
 
     bands = band_copies(part, lambda d: partr.at[d], 0)
     start(bands)
@@ -288,20 +299,28 @@
             fbuf[o, row:row + nz, :] = obuf[o, row:row + nz, :] * cv
             ua[o, row:row + nz, :] = resp0[o, r]
 
-    rim, at = [], 0
-    for yp, third, row, size in tiles():
-        if third or yp < w or yp >= w + ny:
-            rim.append((yp, third, row, size, at))
-            at += size
-    arrived(second)
-    for o in range(orbs):
-        for yp, third, row, size, at in rim:
-            value = padded(None, yr2, zr2, o, yp, third)
-            ua[o, row:row + size, :] = value
-            term = occ_ref[o] * obuf[o, row:row + size, :] * value
-            hp[at:at + size, :] = term if o == 0 else hp[at:at + size, :] + term
-    rims = band_copies(hp, lambda d: hpr.at[d], 2 * (nb - 1))
-    start(rims)
+    rim, parts, at = [], [], 0
+    for which in (0, 1):
+        begin = at
+        for yp, third, row, size in tiles():
+            if third == which and not inside(yp, third):
+                rim.append((yp, third, row, size, at))
+                at += size
+        parts.append((begin, at))
+    rims = []
+    for which, group in ((0, second[4:6]), (1, second[:4] + second[6:])):
+        arrived(group)
+        for o in range(orbs):
+            for yp, third, row, size, at in rim:
+                if third == which:
+                    value = padded(None, yr2, zr2, o, yp, third)
+                    ua[o, row:row + size, :] = value
+                    term = occ_ref[o] * obuf[o, row:row + size, :] * value
+                    hp[at:at + size, :] = term if o == 0 else hp[at:at + size, :] + term
+        begin, end_at = parts[which]
+        piece = pl.ds(begin, end_at - begin)
+        rims += band_copies(hp.at[piece], lambda d: hpr.at[d, piece], (2 + which) * (nb - 1))
+        start(rims[which * (nb - 1):])
     for o in range(orbs):
         for row, size in chunks(*span(1), CHUNK):
             ub[o, row:row + size, :] = relaxed(ua, o, row, size, None)
@@ -322,13 +341,17 @@
     for o in range(orbs):
         sweep(ub, ua, 2, o)
         sweep(ua, ub, 3, o)
-    for o in range(orbs):
-        last(ub, respv, part2, o, range(ny))
-    bands2 = band_copies(part2, lambda d: partr2.at[d], nb - 1)
-    start(bands2)
+    bands2, half = [], ny // 2
+    for i in range(2):
+        for o in range(orbs):
+            last(ub, respv, part2, o, range(i * half, (i + 1) * half))
+        piece = pl.ds(i * half, half)
+        bands2 += band_copies(part2.at[piece], lambda d: partr2.at[d, piece], (1 + 3 * i) * (nb - 1))
+        start(bands2[i * (nb - 1):])
     width = nx // nb
-    arrived(bands2)
     for r in range(ny):
+        if r % half == 0:
+            arrived(bands2[r // half * (nb - 1):][:nb - 1])
         total = part2[r]
         for d in range(nb - 1):
             total = total + partr2[d, r]
@@ -370,7 +393,7 @@
         vmem(orbs, ny, nz, nx), tile, vmem(nb - 1, ny, nz, nx), tile, vmem(nb - 1, ny, nz, nx),
         vmem(rim_rows, nx), vmem(nb - 1, rim_rows, nx),
         wide, wide, wide, wide, wide, wide, vmem(rows, nx),
-        dma(remotes), dma(remotes), dma(3 * (nb - 1)), dma(3 * (nb - 1)), dma(6),
+        dma(remotes), dma(remotes), dma(5 * (nb - 1)), dma(5 * (nb - 1)), dma(6),
     ]
     spec = pl.BlockSpec(memory_space=pltpu.VMEM)
     hbm = pl.BlockSpec(memory_space=pltpu.HBM)

time: 27.3 us -> 26.6 us (0.974)
  Pallas kernels: 26.5 us -> 25.8 us
    pallas_call x1, Pallas kernels: 25.8 us -> 25.1 us  [on_device(): pl.pallas_call(functools.partial(kernel, counts), out_shape=(pltpu.VMEM(o...]
where the time goes in v3:
time: 26.6 us; the launch traced here: 26.5 us
  Pallas kernels  25.8 us (97%)
  between operations  0.64 us (2%)
    pallas_call x1, Pallas kernels, on_device(): pl.pallas_call(functools.partial(kernel, counts), out_shape=(pltpu.VMEM(o...  25.1 us
    pallas_call x1, Pallas kernels, on_device(): pl.pallas_call(store, out_shape=(jax.ShapeDtypeStruct(response.shape, f32...  0.76 us

profile of v3, /device:TPU:0, one launch (start us, length us, event | category | flops | bytes accessed | tf_op | source)
XLA Modules:
  0.0 26.5 jit_solution(18042661434159856189)
XLA Ops:
  0.6 25.1 %shard_map.77 = (f32[2,16,16,128]{3,2,1,0:T(8,128)S(1)}, f32[16,16,64]{2,1,0:T(8,128)S(1)}) custom-call(f32[2]{0:T(128)} %shift_hbm.1, f32[2]{0:T(128)} %occ_hbm.1, f32[2,16,16,128]{3,2,1,0:T(8,128)} %orb_hbm.1, f32[16,16,128]{2,1,0:T(8,128)} %pot_hbm.1, f32[16,16,128]{2,1,0:T(8,128)} %pert_hbm.1, f32[16,16,128]{2,1,0:T(8,128)} %kern_hbm.1), custom_call_target="tpu_custom_call" | custom-call | tf_op jit(solution)/shard_map/pallas_call | solution.py:400
  25.7 0.8 %shard_map.78 = (f32[2,16,16,128]{3,2,1,0:T(8,128)}, f32[16,16,64]{2,1,0:T(8,128)}) custom-call(f32[2,16,16,128]{3,2,1,0:T(8,128)S(1)} %get-tuple-element.4.resp_ref, f32[16,16,64]{2,1,0:T(8,128)S(1)} %get-tuple-element.5.dens_ref), custom_call_target="tpu_custom_call" | custom-call | tf_op jit(solution)/shard_map/pallas_call | solution.py:410
